TPU v7x, 32 devices: a whole 2x2x4 slice. The times are simulated.
32 devices in a mesh: ctx: 16 (over z, y, x), head: 2 (over core).
Axes of the slice: x: 2, y: 2, z: 4, core: 2. Of those that a mesh axis runs over, the one named last changes fastest.
Arguments:
- queries: float32 [8192, 512], P('ctx', 'head'), may hold values from -1024 to 1024
- keys: float32 [8192, 128], P('ctx'), may hold values from -1024 to 1024
- values: float32 [8192, 128], P('ctx'), may hold values from -6 to 6
- cotangent: float32 [8192, 512], P('ctx', 'head'), may hold values from -384 to 384
- source_ids: int32 [8192], P('ctx'), may hold values from 0 to 63
- source_weights: float32 [64], replicated, may hold values from 0.25 to 4
- q_feature: float32 [4, 128, 128], P('head'), may hold values from -4 to 4
- k_feature: float32 [128, 128], replicated, may hold values from -4 to 4
Outputs:
- grad_queries: float32 [8192, 512], P('ctx', 'head')
- grad_keys: float32 [8192, 128], P(('ctx', 'head'))
- grad_values: float32 [8192, 128], P(('ctx', 'head'))
- grad_q_feature: float32 [4, 128, 128], P('head')
- grad_k_feature: float32 [128, 128], replicated
All inputs are finite; a program needn't handle non-finite values.
Results may differ from a plain program's by a relative error of at most 0.0015.
Values sent between devices are 32-bit elements; how exact they have to be, the bound alone decides.
No kernel may reach another device: no remote copies, remote signals or barrier semaphores. Data moves between devices by JAX's collectives and lax.ppermute only.
A program may use at most 64 MiB of HBM per device.

v0:
```python
import jax
import jax.numpy as jnp
from jax import lax
from jax.sharding import PartitionSpec as P


def entering(value, axis, join, neutral, backward):
    count, mine = (lax.axis_size(axis), lax.axis_index(axis))
    pieces = jax.tree.map(lambda part: lax.all_gather(part, axis), value)
    if backward:
        pieces = jax.tree.map(lambda part: part[::-1], pieces)
        mine = count - 1 - mine
    total = jax.tree.map(
        lambda part, zero: jnp.full_like(part, 0) + jnp.asarray(zero, part.dtype), value, neutral
    )

    def turn(position, total):
        longer = join(total, jax.tree.map(lambda part: part[position], pieces))
        return jax.tree.map(lambda new, old: jnp.where(position < mine, new, old), longer, total)

    return lax.fori_loop(0, count - 1, turn, total)


def matmul(left, right):
    return jnp.dot(left, right, precision=lax.Precision.HIGHEST, preferred_element_type=jnp.float32)


def product(form, left, right):
    return jnp.einsum(
        form, left, right, precision=lax.Precision.HIGHEST, preferred_element_type=jnp.float32
    )


def feature_map(inputs, weight):
    logits = matmul(inputs, weight)
    upper = jax.nn.softmax(logits, axis=-1)
    lower = jax.nn.softmax(-logits, axis=-1)
    return (jnp.concatenate([upper, lower], axis=-1), upper, lower)


def feature_back(inputs, weight, upper, lower, grad_feat):
    half = upper.shape[-1]
    grad_upper = grad_feat[:, :half]
    grad_lower = grad_feat[:, half:]
    grad_logits = upper * (grad_upper - jnp.sum(upper * grad_upper, axis=-1, keepdims=True))
    grad_logits = grad_logits - lower * (
        grad_lower - jnp.sum(lower * grad_lower, axis=-1, keepdims=True)
    )
    return (matmul(grad_logits, weight.T), matmul(inputs.T, grad_logits))


def causal_mask(count):
    row_index = lax.broadcasted_iota(jnp.int32, (count, count), 0)
    col_index = lax.broadcasted_iota(jnp.int32, (count, count), 1)
    return (row_index >= col_index).astype(jnp.float32)


def add_pair(earlier, later):
    return (earlier[0] + later[0], earlier[1] + later[1])


def block_terms(query_c, key_c, value_c, scaled_c, prefix, prefix_tot):
    lower_mask = causal_mask(query_c.shape[1])
    scores = product("ncf,ndf->ncd", query_c, key_c) * lower_mask
    numerator = product("ncd,nde->nce", scores, value_c) + product("ncf,nfe->nce", query_c, prefix)
    normalizer = jnp.sum(scores, axis=2) + product("ncf,nf->nc", query_c, prefix_tot)
    output = numerator / normalizer[..., None]
    grad_numer = scaled_c / normalizer[..., None]
    grad_norm = -jnp.sum(scaled_c * output, axis=2) / normalizer
    grad_scores = (product("nce,nde->ncd", grad_numer, value_c) + grad_norm[..., None]) * lower_mask
    grad_query = (
        product("ncd,ndf->ncf", grad_scores, key_c)
        + product("nce,nfe->ncf", grad_numer, prefix)
        + grad_norm[..., None] * prefix_tot[:, None, :]
    )
    grad_key = product("ncd,ncf->ndf", grad_scores, query_c)
    grad_value = product("ncd,nce->nde", scores, grad_numer)
    carried = product("ncf,nce->nfe", query_c, grad_numer)
    carried_totals = product("nc,ncf->nf", grad_norm, query_c)
    return (grad_query, grad_key, grad_value, carried, carried_totals)


def on_device(queries, keys, values, cotangent, source_ids, source_weights, q_feature, k_feature):
    head_count = q_feature.shape[0]
    width = q_feature.shape[1]
    features = 2 * q_feature.shape[2]
    rows = queries.shape[0]
    piece = min(128, rows)
    pieces = rows // piece
    source_index = lax.broadcasted_iota(jnp.int32, (1, source_weights.shape[0]), 1)
    lookup = (source_ids[:, None] == source_index).astype(jnp.float32)
    weight = jnp.sum(lookup * source_weights[None, :], axis=1)
    key_feat, key_upper, key_lower = feature_map(keys, k_feature)
    key_c = key_feat.reshape(pieces, piece, features)
    value_c = values.reshape(pieces, piece, width)
    piece_state = product("ncf,nce->nfe", key_c, value_c)
    piece_tot = jnp.sum(key_c, axis=1)
    share = features // lax.axis_size("head")
    offset = lax.axis_index("head") * share
    slab_feat = lax.dynamic_slice_in_dim(key_feat, offset, share, 1)
    slab_local = (
        lax.dynamic_slice_in_dim(jnp.sum(piece_state, axis=0), offset, share, 0),
        lax.dynamic_slice_in_dim(jnp.sum(piece_tot, axis=0), offset, share, 0),
    )
    slab_zero = (jnp.zeros((share, width), jnp.float32), jnp.zeros((share,), jnp.float32))
    slab_before = entering(slab_local, "ctx", add_pair, slab_zero, False)
    earlier, earlier_totals = (
        lax.all_gather(slab_before[0], "head", axis=0, tiled=True),
        lax.all_gather(slab_before[1], "head", axis=0, tiled=True),
    )
    prefix = jnp.cumsum(piece_state, axis=0) - piece_state + earlier[None]
    prefix_tot = jnp.cumsum(piece_tot, axis=0) - piece_tot + earlier_totals[None]
    grad_keyfeat = jnp.zeros(key_feat.shape, jnp.float32)
    grad_vals = jnp.zeros(values.shape, jnp.float32)
    piece_carried = jnp.zeros((pieces, features, width), jnp.float32)
    piece_carried_tot = jnp.zeros((pieces, features), jnp.float32)
    query_grads = []
    weight_grads = []
    for head in range(head_count):
        query_head = queries[:, head * width : (head + 1) * width]
        query_feat, query_upper, query_lower = feature_map(query_head, q_feature[head])
        scaled = cotangent[:, head * width : (head + 1) * width] * weight[:, None]
        grad_query, grad_key, grad_value, carried, carried_totals = block_terms(
            query_feat.reshape(pieces, piece, features),
            key_c,
            value_c,
            scaled.reshape(pieces, piece, width),
            prefix,
            prefix_tot,
        )
        grad_head, grad_weight = feature_back(
            query_head,
            q_feature[head],
            query_upper,
            query_lower,
            grad_query.reshape(rows, features),
        )
        query_grads.append(grad_head)
        weight_grads.append(grad_weight)
        grad_keyfeat = grad_keyfeat + grad_key.reshape(rows, features)
        grad_vals = grad_vals + grad_value.reshape(rows, width)
        piece_carried = piece_carried + carried
        piece_carried_tot = piece_carried_tot + carried_totals
    carried_all = jnp.sum(piece_carried, axis=0)
    carried_tot = jnp.sum(piece_carried_tot, axis=0)
    inner_later = carried_all[None] - jnp.cumsum(piece_carried, axis=0)
    inner_tot = carried_tot[None] - jnp.cumsum(piece_carried_tot, axis=0)
    grad_keyfeat = grad_keyfeat + (
        product("nce,nfe->ncf", value_c, inner_later) + inner_tot[:, None, :]
    ).reshape(rows, features)
    grad_vals = grad_vals + product("ncf,nfe->nce", key_c, inner_later).reshape(rows, width)
    folded, folded_tot = (
        lax.psum_scatter(carried_all, "head", scatter_dimension=0, tiled=True),
        lax.psum_scatter(carried_tot, "head", scatter_dimension=0, tiled=True),
    )
    later, later_tot = entering((folded, folded_tot), "ctx", add_pair, slab_zero, True)
    slab_grad = matmul(values, later.T) + later_tot[None, :]
    current = lax.dynamic_slice_in_dim(grad_keyfeat, offset, share, 1)
    grad_keyfeat = lax.dynamic_update_slice_in_dim(grad_keyfeat, current + slab_grad, offset, 1)
    grad_vals = grad_vals + matmul(slab_feat, later)
    grad_key_part, grad_kweight = feature_back(keys, k_feature, key_upper, key_lower, grad_keyfeat)
    grad_keys, grad_values = (
        lax.psum_scatter(grad_key_part, "head", scatter_dimension=0, tiled=True),
        lax.psum_scatter(grad_vals, "head", scatter_dimension=0, tiled=True),
    )
    grad_qweight = lax.psum(jnp.stack(weight_grads, axis=0), "ctx")
    grad_kweight = lax.psum(grad_kweight, ("ctx", "head"))
    return (
        jnp.concatenate(query_grads, axis=1),
        grad_keys,
        grad_values,
        grad_qweight,
        grad_kweight,
    )


def solution(mesh):
    placed = (
        P("ctx", "head"),
        P("ctx", None),
        P("ctx", None),
        P("ctx", "head"),
        P("ctx"),
        P(),
        P("head", None, None),
        P(),
    )
    return jax.shard_map(
        on_device,
        mesh=mesh,
        in_specs=placed,
        out_specs=(
            P("ctx", "head"),
            P(("ctx", "head"), None),
            P(("ctx", "head"), None),
            P("head", None, None),
            P(),
        ),
        check_vma=False,
    )
```

profile of v0, /device:TPU:0, one launch (start us, length us, event | category | flops | bytes accessed | tf_op | source)
XLA Modules:
  0.0 441.5 jit_solution(6858536777643410984)
XLA Ops:
  7.2 1.4 fusion.102
  11.2 0.9 copy.142
  12.1 0.9 copy.157
  16.1 42.4 %all-gather.4 = f32[16,1,128]{2,1,0:T(1,128)S(1)} all-gather(f32[1,1,128]{2,1,0:T(1,128)S(1)} %dynamic-slice_bitcast_fusion.1), channel_id=3, replica_groups=mesh['ctx'=16,'head'=2] {'ctx'}, dimensions={0}, use_global_device_ids=true | all-gather | bytes 8704 | tf_op jit(solution)/shard_map/all_gather | solution.py:9
  59.9 1.8 fusion.107
  61.7 1.8 fusion.109
  63.4 5.7 %all-gather.10.cloned.1.call-done = f32[2048,128]{1,0:T(8,128)} async-done(((f32[128,128]{1,0:T(8,128)}), f32[2048,128]{1,0:T(8,128)}) %all-gather.10.cloned.1.call-update) | async-done | bytes 1048592 | tf_op jit(solution)/shard_map/all_gather | solution.py:9
  69.2 13.6 %while.32 = (s32[]{:T(128)}, f32[128,128]{1,0:T(8,128)S(1)}, f32[128]{0:T(128)S(1)}, s32[]{:T(128)}, f32[16,128,128]{2,1,0:T(8,128)}, /*index=5*/f32[16,128]{1,0:T(8,128)S(1)}, s32[]{:T(128)}, s32[]{:T(128)}) while((s32[]{:T(128)}, f32[128,128]{1,0:T(8,128)S(1)}, f32[128]{0:T(128)S(1)}, s32[]{:T(128)}, ...), condition=%wide.region_15.16_spmd.clone, body=%wide.region_14.15_spmd.clone.sunk | while | flops 49540 | bytes 198267 | solution.py:21
  69.2 0.9 add_select_fusion.4
  70.1 0.9 add_select_fusion.4
  71.0 0.9 add_select_fusion.4
  71.9 0.9 add_select_fusion.4
  72.8 0.9 add_select_fusion.4
  73.7 0.9 add_select_fusion.4
  74.7 0.9 add_select_fusion.4
  75.6 0.9 add_select_fusion.4
  76.5 0.9 add_select_fusion.4
  77.4 0.9 add_select_fusion.4
  78.3 0.9 add_select_fusion.4
  79.2 0.9 add_select_fusion.4
  80.1 0.9 add_select_fusion.4
  81.0 0.9 add_select_fusion.4
  81.9 0.9 add_select_fusion.4
  82.8 1.8 all-gather.5
  84.8 1.0 fusion.22
  85.8 1.0 fusion.42
  86.8 2.1 all_gather.35
  88.9 1.1 fusion.20
  90.0 1.1 fusion.40
  93.0 1.4 fusion.45
  94.4 1.4 fusion.33
  95.9 1.4 fusion.36
  100.2 2.5 all-reduce
  103.7 1.4 convolution_add_fusion.2
  105.8 0.8 fusion.106
  107.7 0.8 fusion.105
  108.9 2.1 fusion.110
  111.1 1.2 reduce-window_subtract_fusion
  112.3 1.4 fusion.2
  113.7 3.9 reduce-scatter.4.cloned.1.call-done
  117.8 41.0 %all-gather.6 = f32[16,1,128]{2,1,0:T(1,128)S(1)} all-gather(f32[1,1,128]{2,1,0:T(1,128)S(1)} %dynamic-slice_bitcast_fusion), channel_id=5, replica_groups=mesh['ctx'=16,'head'=2] {'ctx'}, dimensions={0}, use_global_device_ids=true | all-gather | bytes 8704 | tf_op jit(solution)/shard_map/all_gather | solution.py:9
  158.8 1.8 copy.212
  160.7 0.8 copy.213
  161.6 0.9 copy.210
  162.5 1.2 copy.209
  163.7 1.8 copy.211
  165.5 1.2 multiply_reduce_fusion.2
  166.8 0.9 copy-done.13
  171.2 1.0 fusion.28
  173.0 3.7 all-gather.12.cloned.1.call-done
  176.7 1.3 rev.6
  178.0 1.0 while.33
  179.6 0.8 copy-done.19
  180.5 1.0 convolution_bitcast_fusion
  181.6 1.3 convolution_add_fusion.5
  183.7 1.3 fusion.111
  185.0 0.9 copy-done.4
  186.8 1.0 copy.180
  187.8 99.0 %all-reduce.4.cloned.1.call-done = f32[2,128,128]{1,2,0:T(8,128)} async-done(((f32[2,128,128]{1,2,0:T(8,128)}), f32[2,128,128]{1,2,0:T(8,128)}) %all-reduce.4.cloned.1.call-update) | async-done | bytes 131088 | tf_op jit(solution)/shard_map/psum | solution.py:166
  286.8 1.7 copy.181
  288.4 122.9 %all-reduce.6.cloned.1.call-done = f32[128,128]{0,1:T(8,128)} async-done(((f32[128,128]{0,1:T(8,128)}), f32[128,128]{0,1:T(8,128)}) %all-reduce.6.cloned.1.call-update) | async-done | bytes 65552 | tf_op jit(solution)/shard_map/psum | solution.py:167
  411.3 1.6 copy.182
  412.8 10.1 %reduce-scatter.8.cloned.1.call-done = f32[256,128]{1,0:T(8,128)} async-done(((f32[512,128]{1,0:T(8,128)}), f32[256,128]{1,0:T(8,128)}) %reduce-scatter.8.cloned.1.call-update) | async-done | bytes 131088 | tf_op jit(solution)/shard_map/reduce_scatter | solution.py:164
  422.9 11.7 %reduce-scatter.6.cloned.1.call-done = f32[256,128]{1,0:T(8,128)} async-done(((f32[512,128]{1,0:T(8,128)}), f32[256,128]{1,0:T(8,128)}) %reduce-scatter.6.cloned.1.call-update) | async-done | bytes 131088 | tf_op jit(solution)/shard_map/reduce_scatter | solution.py:163
  (197 shorter events, 22.3 us)
Async XLA Ops:
  7.2 1.8 copy-start
  7.2 62.0 %all-gather.10.cloned.1.call-start = ((), (), s32[]{:S(2)}) async-start(), calls=%async_computation.8 | async-start | bytes 1114112 | tf_op jit(solution)/shard_map/all_gather | solution.py:9
  9.0 2.0 copy-start.29
  10.3 0.7 copy-start.38
  10.3 0.7 copy-start.39
  10.3 107.3 %reduce-scatter.4.cloned.1.call-start = ((), (), s32[]{:S(2)}) async-start(), calls=%async_computation.3 | async-start | bytes 196608 | tf_op jit(solution)/shard_map/reduce_scatter | solution.py:153
  13.1 45.4 %copy-start.12 = (f32[512,256]{1,0:T(8,128)S(1)}, f32[512,256]{1,0:T(8,128)}, u32[]{:S(2)}) copy-start(f32[512,256]{1,0:T(8,128)} %param.12) | copy-start | bytes 1572868
  13.5 0.7 copy-start.14
  13.5 45.1 %copy-start.27 = (f32[2,128,128]{2,1,0:T(8,128)S(1)}, f32[2,128,128]{2,1,0:T(8,128)}, u32[]{:S(2)}) copy-start(f32[2,128,128]{2,1,0:T(8,128)} %param.18) | copy-start | bytes 393220
  14.2 0.7 copy-start.40
  58.6 3.1 copy-start.24
  69.2 15.4 %copy-start.15 = (f32[4,256]{0,1:T(8,128)S(1)}, f32[4,256]{0,1:T(8,128)}, u32[]{:S(2)}) copy-start(f32[4,256]{0,1:T(8,128)} %copy-done.14) | copy-start | bytes 12292
  90.0 1.8 copy-start.16
  90.0 1.8 copy-start.31
  91.1 0.7 copy-start.37
  91.8 4.1 copy-start.33
  91.8 0.8 copy-start.25
  95.9 2.1 copy-start.1
  95.9 2.1 copy-start.20
  97.3 0.7 copy-start.36
  102.6 1.0 copy-start.11
  105.7 1.2 copy-start.10
  105.7 1.3 copy-start.17
  105.7 1.3 copy-start.34
  107.7 1.2 copy-start.26
  111.0 65.7 %all-gather.12.cloned.1.call-start = ((), (), s32[]{:S(2)}) async-start(), calls=%async_computation.9 | async-start | bytes 1114112 | tf_op jit(solution)/shard_map/all_gather | solution.py:9
  111.1 1.2 copy-start.9
  117.6 169.1 %all-reduce.4.cloned.1.call-start = ((), (), s32[]{:S(2)}) async-start(), calls=%async_computation.6 | async-start | bytes 262144 | tf_op jit(solution)/shard_map/psum | solution.py:166
  158.8 1.9 copy-start.22
  160.6 1.0 copy-start.23
  165.5 1.2 copy-start.7
  165.5 1.2 copy-start.8
  166.7 1.0 copy-start.13
  167.7 0.7 copy-start.3
  167.7 1.0 copy-start.5
  167.7 1.1 copy-start.6
  169.1 1.1 copy-start.32
  169.5 1.0 copy-start.18
  171.2 1.1 copy-start.2
  171.2 1.1 copy-start.21
  173.0 238.3 %all-reduce.6.cloned.1.call-start = ((), (), s32[]{:S(2)}) async-start(), calls=%async_computation.7 | async-start | bytes 131072 | tf_op jit(solution)/shard_map/psum | solution.py:167
  176.7 1.3 copy-start.35
  179.5 1.0 copy-start.19
  181.5 241.4 %reduce-scatter.8.cloned.1.call-start = ((), (), s32[]{:S(2)}) async-start(), calls=%async_computation.5 | async-start | bytes 393216 | tf_op jit(solution)/shard_map/reduce_scatter | solution.py:164
  182.9 0.8 copy-start.30
  182.9 251.7 %reduce-scatter.6.cloned.1.call-start = ((), (), s32[]{:S(2)}) async-start(), calls=%async_computation.4 | async-start | bytes 393216 | tf_op jit(solution)/shard_map/reduce_scatter | solution.py:163
  183.7 1.3 copy-start.28
  185.0 0.9 copy-start.4
Sparse Core Ops, SparseCore 0:
  11.3 57.8 all-gather.9
  111.1 6.4 reduce-scatter.3
  120.4 56.2 all-gather.11
  182.6 104.1 all-reduce.3
  292.8 118.4 all-reduce.5
  413.9 8.9 reduce-scatter.7
  425.7 8.8 reduce-scatter.5
where the time goes:
time: 443 us; the launch traced here: 441 us
  waiting for transfers between devices  257 us (58%)
  blocking collectives  89.8 us (20%)
  matrix products  32.6 us (7%)
  local copies, waits for them, and re-layouts  26.5 us (6%)
  other arithmetic  19 us (4%)
  between operations  15.4 us (3%)
    psum x1, waiting for transfers between devices, on_device(): grad_kweight = lax.psum(grad_kweight, ('ctx', 'head'))  123 us
    psum x1, waiting for transfers between devices, on_device(): grad_qweight = lax.psum(jnp.stack(weight_grads, axis=0), 'ctx')  99 us
    all_gather x2, blocking collectives, entering(): pieces = jax.tree.map(lambda part: lax.all_gather(part, axis), value)  83.5 us
    dot_general x25, matrix products, product(): jnp.einsum(form, left, right, precision=lax.Precision.HIGHEST, preferred_...  24.8 us
    unnamed x92, local copies, waits for them, and re-layouts  19.6 us
    select_n x60, other arithmetic, turn(): jnp.where(position < mine, new, old)  13.7 us
    reduce_scatter x1, waiting for transfers between devices, on_device(): lax.psum_scatter(grad_key_part, 'head', scatter_dimension=0, tiled=True)  11.7 us
    reduce_scatter x1, waiting for transfers between devices, on_device(): lax.psum_scatter(grad_vals, 'head', scatter_dimension=0, tiled=True)  10.1 us
  transfers between devices with their start and end apart: 7, of which 7 were waited for; matrix products, arithmetic and copies ran while one was open for 8% of the time, Pallas kernels for 0%

commit v1 on v0

--- a/solution.py
+++ b/solution.py
@@ -2,6 +2,7 @@
 import jax.numpy as jnp
 from jax import lax
 from jax.sharding import PartitionSpec as P
+from jax.lax import psum
 
 
 def entering(value, axis, join, neutral, backward):
@@ -164,7 +165,15 @@
         lax.psum_scatter(grad_vals, "head", scatter_dimension=0, tiled=True),
     )
     grad_qweight = lax.psum(jnp.stack(weight_grads, axis=0), "ctx")
-    grad_kweight = lax.psum(grad_kweight, ("ctx", "head"))
+
+    def match_cubes(field):
+        mesh_dim = "ctx"
+        ax_name = "head"
+        for dev_j in (ax_name, mesh_dim):
+            field = psum(field, axis_name=dev_j)
+        return field
+
+    grad_kweight = match_cubes(grad_kweight)
     return (
         jnp.concatenate(query_grads, axis=1),
         grad_keys,

time: 443 us -> 406 us (0.916)
  waiting for transfers between devices: 257 us -> 196 us
  other arithmetic: 19 us -> 41.9 us
    psum x1, waiting for transfers between devices: 123 us -> 16 us  [match_cubes(): field = psum(field, axis_name=dev_j)]
    all_gather x2, waiting for transfers between devices: 9.41 us -> 52.2 us  [entering(): pieces = jax.tree.map(lambda part: lax.all_gather(part, axis), value)]
    select_n x60, other arithmetic: 13.7 us -> 36.6 us  [turn(): jnp.where(position < mine, new, old)]
    psum x1, waiting for transfers between devices: 99 us -> 109 us  [on_device(): grad_qweight = lax.psum(jnp.stack(weight_grads, axis=0), 'ctx')]
    unnamed x92 -> x80, local copies, waits for them, and re-layouts: 19.6 us -> 17.5 us
  transfers between devices with their start and end apart: 7 -> 7, of which waited for: 7 -> 7; matrix products, arithmetic and copies ran while one was open for 8% -> 7% of each run, Pallas kernels for 0% -> 0%
where the time goes in v1:
time: 406 us; the launch traced here: 404 us
  waiting for transfers between devices  196 us (48%)
  blocking collectives  87.3 us (22%)
  other arithmetic  41.9 us (10%)
  matrix products  34.6 us (9%)
  local copies, waits for them, and re-layouts  26.9 us (7%)
  between operations  15.3 us (4%)
    psum x1, waiting for transfers between devices, on_device(): grad_qweight = lax.psum(jnp.stack(weight_grads, axis=0), 'ctx')  109 us
    all_gather x2, blocking collectives, entering(): pieces = jax.tree.map(lambda part: lax.all_gather(part, axis), value)  80.9 us
    all_gather x2, waiting for transfers between devices, entering(): pieces = jax.tree.map(lambda part: lax.all_gather(part, axis), value)  52.2 us
    select_n x60, other arithmetic, turn(): jnp.where(position < mine, new, old)  36.6 us
    dot_general x25, matrix products, product(): jnp.einsum(form, left, right, precision=lax.Precision.HIGHEST, preferred_...  26.7 us
    unnamed x80, local copies, waits for them, and re-layouts  17.5 us
    psum x1, waiting for transfers between devices, match_cubes(): field = psum(field, axis_name=dev_j)  16 us
    reduce_scatter x1, waiting for transfers between devices, on_device(): lax.psum_scatter(grad_key_part, 'head', scatter_dimension=0, tiled=True)  11.7 us
  transfers between devices with their start and end apart: 7, of which 7 were waited for; matrix products, arithmetic and copies ran while one was open for 7% of the time, Pallas kernels for 0%

profile of v1, /device:TPU:0, one launch (start us, length us, event | category | flops | bytes accessed | tf_op | source)
XLA Modules:
  0.0 403.6 jit_solution(6624324895267392985)
XLA Ops:
  7.2 1.4 fusion.102
  11.2 0.9 copy.142
  15.7 42.4 %all-gather.4 = f32[16,1,128]{2,1,0:T(1,128)S(1)} all-gather(f32[1,1,128]{2,1,0:T(1,128)S(1)} %dynamic-slice_bitcast_fusion.1), channel_id=3, replica_groups=mesh['ctx'=16,'head'=2] {'ctx'}, dimensions={0}, use_global_device_ids=true | all-gather | bytes 8704 | tf_op jit(solution)/shard_map/all_gather | solution.py:10
  59.4 1.8 fusion.107
  61.2 1.8 fusion.109
  63.0 6.2 %all-gather.10.cloned.1.call-done = f32[2048,128]{1,0:T(8,128)} async-done(((f32[128,128]{1,0:T(8,128)}), f32[2048,128]{1,0:T(8,128)}) %all-gather.10.cloned.1.call-update) | async-done | bytes 1048592 | tf_op jit(solution)/shard_map/all_gather | solution.py:10
  69.2 13.6 %while.32 = (s32[]{:T(128)}, f32[128,128]{1,0:T(8,128)S(1)}, f32[128]{0:T(128)S(1)}, s32[]{:T(128)}, f32[16,128,128]{2,1,0:T(8,128)}, /*index=5*/f32[16,128]{1,0:T(8,128)S(1)}, s32[]{:T(128)}, s32[]{:T(128)}) while((s32[]{:T(128)}, f32[128,128]{1,0:T(8,128)S(1)}, f32[128]{0:T(128)S(1)}, s32[]{:T(128)}, ...), condition=%wide.region_15.16_spmd.clone, body=%wide.region_14.15_spmd.clone.sunk | while | flops 49540 | bytes 198267 | solution.py:22
  69.2 0.9 add_select_fusion.4
  70.1 0.9 add_select_fusion.4
  71.0 0.9 add_select_fusion.4
  71.9 0.9 add_select_fusion.4
  72.8 0.9 add_select_fusion.4
  73.7 0.9 add_select_fusion.4
  74.6 0.9 add_select_fusion.4
  75.5 0.9 add_select_fusion.4
  76.4 0.9 add_select_fusion.4
  77.4 0.9 add_select_fusion.4
  78.3 0.9 add_select_fusion.4
  79.2 0.9 add_select_fusion.4
  80.1 0.9 add_select_fusion.4
  81.0 0.9 add_select_fusion.4
  81.9 0.9 add_select_fusion.4
  82.8 1.8 all-gather.5
  84.7 1.0 fusion.22
  85.7 1.0 fusion.42
  86.8 2.1 all_gather.35
  88.9 1.1 fusion.20
  90.0 1.1 fusion.40
  92.8 1.4 fusion.45
  94.2 1.4 fusion.33
  95.6 1.4 fusion.36
  99.9 2.5 all-reduce
  102.4 38.5 %all-gather.6 = f32[16,1,128]{2,1,0:T(1,128)S(1)} all-gather(f32[1,1,128]{2,1,0:T(1,128)S(1)} %dynamic-slice_bitcast_fusion), channel_id=5, replica_groups=mesh['ctx'=16,'head'=2] {'ctx'}, dimensions={0}, use_global_device_ids=true | all-gather | bytes 8704 | tf_op jit(solution)/shard_map/all_gather | solution.py:10
  142.6 1.4 convolution_add_fusion.2
  146.3 1.8 copy.213
  148.1 2.6 fusion.4
  150.7 2.1 fusion.110
  152.9 1.2 reduce-window_subtract_fusion
  154.1 1.4 fusion.2
  155.5 0.9 reduce-scatter.4.cloned.1.call-done
  156.7 1.8 fusion.105
  159.3 1.2 copy.209
  160.6 1.8 copy.211
  162.4 1.2 multiply_reduce_fusion.2
  163.7 0.9 copy-done.12
  167.7 1.1 fusion.28
  169.4 46.0 %all-gather.12.cloned.1.call-done = f32[2048,128]{1,0:T(8,128)} async-done(((f32[128,128]{1,0:T(8,128)}), f32[2048,128]{1,0:T(8,128)}) %all-gather.12.cloned.1.call-update) | async-done | bytes 1048592 | tf_op jit(solution)/shard_map/all_gather | solution.py:10
  215.4 2.4 rev.6
  217.8 23.7 %while.33 = (s32[]{:T(128)}, f32[128,128]{1,0:T(8,128)S(1)}, f32[128]{0:T(128)S(1)}, s32[]{:T(128)}, f32[16,128,128]{2,1,0:T(8,128)}, /*index=5*/f32[16,128]{1,0:T(8,128)}, s32[]{:T(128)}, s32[]{:T(128)}) while((s32[]{:T(128)}, f32[128,128]{1,0:T(8,128)S(1)}, f32[128]{0:T(128)S(1)}, s32[]{:T(128)}, f32[16,128,128]{2,1,0:T(8,128)}, ...), condition=%wide.region_35.36_spmd.clone, body=%wide.region_34.35_spmd.clone.sunk | while | flops 49540 | bytes 198267 | solution.py:22
  218.5 0.9 add_select_fusion.5
  220.1 0.9 add_select_fusion.5
  224.8 0.9 add_select_fusion.5
  226.4 0.9 add_select_fusion.5
  228.0 0.9 add_select_fusion.5
  243.0 1.0 convolution_bitcast_fusion
  244.7 16.0 %all-reduce.5.cloned.1.call-done = f32[128,128]{0,1:T(8,128)} async-done(((f32[128,128]{0,1:T(8,128)}), f32[128,128]{0,1:T(8,128)}) %all-reduce.5.cloned.1.call-update) | async-done | bytes 65552 | tf_op jit(solution)/shard_map/psum | solution.py:173
  260.8 1.3 convolution_add_fusion.5
  262.9 1.3 fusion.111
  264.3 0.9 copy-done.4
  266.0 1.0 copy.180
  267.0 108.6 %all-reduce.7.cloned.1.call-done = (f32[2,128,128]{1,2,0:T(8,128)}, f32[128,128]{0,1:T(8,128)}) async-done(((f32[2,128,128]{1,2,0:T(8,128)}, f32[128,128]{0,1:T(8,128)}), (f32[2,128,128]{1,2,0:T(8,128)}, f32[128,128]{0,1:T(8,128)})) %all-reduce.7.cloned.1.call-update) | async-done | bytes 196624 | tf_op jit(solution)/shard_map/psum | solution.py:167
  375.6 1.7 copy.181
  378.0 7.0 %reduce-scatter.8.cloned.1.call-done = f32[256,128]{1,0:T(8,128)} async-done(((f32[512,128]{1,0:T(8,128)}), f32[256,128]{1,0:T(8,128)}) %reduce-scatter.8.cloned.1.call-update) | async-done | bytes 131088 | tf_op jit(solution)/shard_map/reduce_scatter | solution.py:165
  385.1 11.7 %reduce-scatter.6.cloned.1.call-done = f32[256,128]{1,0:T(8,128)} async-done(((f32[512,128]{1,0:T(8,128)}), f32[256,128]{1,0:T(8,128)}) %reduce-scatter.6.cloned.1.call-update) | async-done | bytes 131088 | tf_op jit(solution)/shard_map/reduce_scatter | solution.py:164
  (185 shorter events, 44.6 us)
Async XLA Ops:
  7.2 1.8 copy-start
  7.2 62.0 %all-gather.10.cloned.1.call-start = ((), (), s32[]{:S(2)}) async-start(), calls=%async_computation.7 | async-start | bytes 1114112 | tf_op jit(solution)/shard_map/all_gather | solution.py:10
  9.0 2.0 copy-start.22
  10.3 0.7 copy-start.32
  10.3 0.7 copy-start.33
  10.3 146.1 %reduce-scatter.4.cloned.1.call-start = ((), (), s32[]{:S(2)}) async-start(), calls=%async_computation.3 | async-start | bytes 196608 | tf_op jit(solution)/shard_map/reduce_scatter | solution.py:154
  13.1 45.0 %copy-start.11 = (f32[512,256]{1,0:T(8,128)S(1)}, f32[512,256]{1,0:T(8,128)}, u32[]{:S(2)}) copy-start(f32[512,256]{1,0:T(8,128)} %param.12) | copy-start | bytes 1572868
  13.5 44.6 %copy-start.20 = (f32[2,128,128]{2,1,0:T(8,128)S(1)}, f32[2,128,128]{2,1,0:T(8,128)}, u32[]{:S(2)}) copy-start(f32[2,128,128]{2,1,0:T(8,128)} %param.18) | copy-start | bytes 393220
  13.7 0.7 copy-start.34
  90.0 1.8 copy-start.13
  90.0 1.8 copy-start.24
  91.1 0.7 copy-start.31
  91.7 3.9 copy-start.27
  95.6 2.1 copy-start.1
  95.6 2.1 copy-start.17
  97.0 0.7 copy-start.30
  141.6 1.0 copy-start.10
  146.3 1.8 copy-start.14
  146.3 1.8 copy-start.28
  148.1 2.6 copy-start.19
  152.8 62.6 %all-gather.12.cloned.1.call-start = ((), (), s32[]{:S(2)}) async-start(), calls=%async_computation.8 | async-start | bytes 1114112 | tf_op jit(solution)/shard_map/all_gather | solution.py:10
  152.8 1.2 copy-start.9
  156.4 104.3 %all-reduce.5.cloned.1.call-start = ((), (), s32[]{:S(2)}) async-start(), calls=%async_computation.6 | async-start | bytes 131072 | tf_op jit(solution)/shard_map/psum | solution.py:173
  162.4 1.2 copy-start.5
  162.4 1.2 copy-start.6
  163.6 1.0 copy-start.12
  164.6 0.7 copy-start.3
  164.6 1.0 copy-start.7
  164.6 1.1 copy-start.8
  165.9 1.0 copy-start.15
  166.0 1.0 copy-start.25
  167.7 1.1 copy-start.2
  167.7 1.1 copy-start.18
  215.4 2.4 copy-start.29
  242.0 1.0 copy-start.16
  244.0 131.6 %all-reduce.7.cloned.1.call-start = ((), (), s32[]{:S(2)}) async-start(), calls=%async_computation.9 | async-start | bytes 393216 | tf_op jit(solution)/shard_map/psum | solution.py:167
  260.7 124.3 %reduce-scatter.8.cloned.1.call-start = ((), (), s32[]{:S(2)}) async-start(), calls=%async_computation.5 | async-start | bytes 393216 | tf_op jit(solution)/shard_map/reduce_scatter | solution.py:165
  262.1 0.8 copy-start.23
  262.1 134.6 %reduce-scatter.6.cloned.1.call-start = ((), (), s32[]{:S(2)}) async-start(), calls=%async_computation.4 | async-start | bytes 393216 | tf_op jit(solution)/shard_map/reduce_scatter | solution.py:164
  262.9 1.3 copy-start.21
  264.2 0.9 copy-start.4
  375.6 1.7 copy-start.26
Sparse Core Ops, SparseCore 0:
  11.3 57.8 all-gather.9
  152.9 3.4 reduce-scatter.3
  159.2 56.1 all-gather.11
  244.1 16.5 all-reduce.4
  266.4 109.1 all-reduce.6
  378.3 6.7 reduce-scatter.7
  387.9 8.8 reduce-scatter.5
